TPU v7x, 128 devices: a whole 4x4x4 slice. The times are simulated.
128 devices in a mesh: sect: 2 (over core), grp: 8 (over x, z_hi), dev: 8 (over z_lo, y).
Axes of the slice: x: 4, y: 4, z: 4 (z_hi: 2, z_lo: 2; z = z_hi * 2 + z_lo), core: 2. Of those that a mesh axis runs over, the one named last changes fastest.
Arguments:
- tokens: bfloat16 [512, 7168], P(('sect', 'grp', 'dev')), may hold values from -6 to 6
- expert_ids: int32 [512, 8], P(('sect', 'grp', 'dev')), may hold values from 0 to 31, all different within a row; in each aligned block of 4 rows (0 to 3, 4 to 7, ...) at most 2 rows name the same one
- gate_weights: float32 [512, 8], P(('sect', 'grp', 'dev')), may hold values from 0.1 to 0.6
- w_gate: bfloat16 [32, 7168, 2048], P(('sect', 'grp'), None, 'dev'), may hold values from -0.0625 to 0.0625
- w_up: bfloat16 [32, 7168, 2048], P(('sect', 'grp'), None, 'dev'), may hold values from -0.0625 to 0.0625
- w_down: bfloat16 [32, 2048, 7168], P(('sect', 'grp'), 'dev'), may hold values from -0.125 to 0.125
Outputs:
- mixed: bfloat16 [512, 7168], P(('sect', 'grp', 'dev'))
Inputs may be any that keep to these rules, and one draw needn't show every extreme that they name: `expert_ids`: each row names 8 different experts. Within the 4 rows of one device no expert is named by more than 2 rows, and on some device some expert is named by exactly 2.
All inputs are finite; a program needn't handle non-finite values.
Results may differ from a plain program's by a relative error of at most 0.015.
Values may be sent and summed in bfloat16 or wider, within the bound.
A program may use at most 128 MiB of HBM per device.

v0:
```python
import jax
import jax.numpy as jnp
from jax import lax
from jax.sharding import PartitionSpec as P

TOP = 8
CAP = 2


def body(tokens, expert_ids, gate_weights, w_gate, w_up, w_down):
    groups = lax.axis_size(("sect", "grp"))
    lane_count = lax.axis_size("dev")
    row_count, model_width = tokens.shape
    local_experts = w_gate.shape[0]
    expert_count = groups * local_experts
    slot_count = expert_count * CAP
    catalog = jnp.arange(expert_count, dtype=jnp.int32)
    per_row = jnp.sum((expert_ids[:, :, None] == catalog[None, None, :]).astype(jnp.int32), axis=1)
    earlier = jnp.cumsum(per_row, axis=0) - per_row
    slot_of = expert_ids * CAP + jnp.take_along_axis(earlier, expert_ids, axis=1)
    positions = jnp.arange(slot_count, dtype=jnp.int32)
    placing = jnp.sum(
        (slot_of[:, :, None] == positions[None, None, :]).astype(jnp.bfloat16), axis=1
    )
    outbound = jnp.dot(placing.T, tokens, preferred_element_type=jnp.float32).astype(jnp.bfloat16)
    outbound = outbound.reshape(groups, 1, local_experts, CAP, model_width)
    copies = jnp.broadcast_to(outbound, (groups, lane_count, local_experts, CAP, model_width))
    copies = copies.reshape(groups * lane_count, local_experts, CAP, model_width)
    arrived = lax.all_to_all(
        copies, ("sect", "grp", "dev"), split_axis=0, concat_axis=0, tiled=True
    )
    arrived = arrived.reshape(groups, lane_count, local_experts, CAP, model_width)
    gate_proj = jnp.einsum("abjcd,jdf->jabcf", arrived, w_gate, preferred_element_type=jnp.float32)
    up_proj = jnp.einsum("abjcd,jdf->jabcf", arrived, w_up, preferred_element_type=jnp.float32)
    hidden = (jax.nn.silu(gate_proj) * up_proj).astype(jnp.bfloat16)
    partial_value = jnp.einsum(
        "jabcf,jfd->abjcd", hidden, w_down, preferred_element_type=jnp.float32
    ).astype(jnp.bfloat16)
    flattened = partial_value.reshape(groups * lane_count, local_experts, CAP, model_width)
    returned = lax.all_to_all(
        flattened, ("sect", "grp", "dev"), split_axis=0, concat_axis=0, tiled=True
    )
    returned = returned.reshape(groups, lane_count, local_experts, CAP, model_width)
    expert_out = jnp.sum(returned.astype(jnp.float32), axis=1).astype(jnp.bfloat16)
    slot_rows = expert_out.reshape(slot_count, model_width)
    picked = jnp.take(slot_rows, slot_of.reshape(-1), axis=0).reshape(row_count, TOP, model_width)
    mixed = jnp.sum(gate_weights[:, :, None] * picked.astype(jnp.float32), axis=1)
    return mixed.astype(jnp.bfloat16)


def solution(mesh):
    in_specs = (
        P(("sect", "grp", "dev"), None),
        P(("sect", "grp", "dev"), None),
        P(("sect", "grp", "dev"), None),
        P(("sect", "grp"), None, "dev"),
        P(("sect", "grp"), None, "dev"),
        P(("sect", "grp"), "dev", None),
    )
    out_specs = P(("sect", "grp", "dev"), None)
    return jax.shard_map(body, mesh=mesh, in_specs=in_specs, out_specs=out_specs, check_vma=False)
```

profile of v0, /device:TPU:1, one launch (start us, length us, event | category | flops | bytes accessed | tf_op | source)
XLA Modules:
  0.0 284.6 jit_solution(14850840383848614110)
XLA Ops:
  0.0 0.0 copy-start
  0.0 0.8 convert_reduce_fusion
  0.8 0.7 bitcast_or_fusion
  1.5 0.1 reshape.87
  1.6 0.8 gather_fusion.1
  2.3 0.1 reshape.90
  2.4 0.7 compare_and_fusion
  3.1 0.1 fusion.19
  3.2 0.0 copy-done
  3.2 0.5 convolution_convert_fusion.1
  3.7 0.3 broadcast_in_dim.28
  4.0 4.7 %broadcast_in_dim.29 = bf16[16,8,2,2,7168]{4,3,2,1,0:T(2,128)(2,1)S(1)} broadcast(bf16[16,2,2,7168]{3,2,1,0:T(2,128)(2,1)S(1)} %broadcast_in_dim.28), dimensions={0,2,3,4} | broadcast | bytes 8257536 | tf_op jit(solution)/shard_map/broadcast_in_dim | solution.py:27
  8.7 101.4 %all_to_all.10 = bf16[128,2,2,7168]{3,2,1,0:T(2,128)(2,1)S(1)} all-to-all(bf16[128,2,2,7168]{3,2,1,0:T(2,128)(2,1)S(1)} %bitcast.47), channel_id=1, replica_groups=mesh['sect'=2,'grp'=8,'dev'=8] {'sect','grp','dev'}, dimensions={0} | all-to-all | bytes 14680064 | tf_op jit(solution)/shard_map/all_to_all | solution.py:29
  110.2 4.5 %fusion.4 = f32[2,16,8,2,256]{4,2,3,1,0:T(8,128)S(1)} fusion(bf16[2,7168,256]{2,1,0:T(8,128)(2,1)} %param.9, bf16[128,2,2,7168]{3,2,1,0:T(2,128)(2,1)S(1)} %all_to_all.10), kind=kOutput, calls=%fused_computation.8 | convolution fusion | flops 1879048192 | bytes 15204352 | tf_op jit(solution)/shard_map/abjcd,jdf->jabcf/dot_general | solution.py:33
  114.7 5.5 %fusion.13 = bf16[2,16,8,2,256]{4,2,3,1,0:T(8,128)(2,1)S(1)} fusion(bf16[2,7168,256]{2,1,0:T(8,128)(2,1)} %param.10, f32[2,16,8,2,256]{4,2,3,1,0:T(8,128)S(1)} %fusion.4, bf16[128,2,2,7168]{3,2,1,0:T(2,128)(2,1)S(1)} %all_to_all.10), kind=kOutput, calls=%fused_computation.16 | convolution fusion | flops 1879834624 | bytes 15466496 | tf_op jit(solution)/shard_map/abjcd,jdf->jabcf/dot_general | solution.py:34
  120.2 8.1 %fusion = bf16[16,8,2,2,7168]{4,1,3,0,2:T(8,128)(2,1)} fusion(bf16[2,16,8,2,256]{4,2,3,1,0:T(8,128)(2,1)S(1)} %fusion.13, bf16[2,256,7168]{2,1,0:T(8,128)(2,1)} %param.11), kind=kOutput, calls=%fused_computation.3 | convolution fusion | flops 1882718208 | bytes 14942208 | tf_op jit(solution)/shard_map/jabcf,jfd->abjcd/dot_general | solution.py:36
  128.3 3.7 %copy.42 = bf16[16,8,2,2,7168]{4,1,0,3,2:T(8,128)(2,1)S(1)} copy(bf16[16,8,2,2,7168]{4,1,3,0,2:T(8,128)(2,1)} %fusion) | data formatting | bytes 14680064 | tf_op jit(solution)/shard_map/convert_element_type | solution.py:38
  132.0 28.1 %copy.21 = bf16[128,2,2,7168]{3,2,1,0:T(2,128)(2,1)} copy(bf16[128,2,2,7168]{3,0,2,1:T(8,128)(2,1)S(1)} %bitcast.46) | data formatting | bytes 14680064 | tf_op jit(solution)/shard_map/reshape | solution.py:39
  160.1 14.6 %all-to-all-start.1 = ((bf16[128,2,2,7168]{3,2,1,0:T(2,128)(2,1)}), bf16[128,2,2,7168]{3,2,1,0:T(2,128)(2,1)}, u32[]{:S(2)}, u32[]{:S(2)}) async-start(bf16[128,2,2,7168]{3,2,1,0:T(2,128)(2,1)} %copy.21), calls=%async_computation.1 | async-start | bytes 14680064 | tf_op jit(solution)/shard_map/all_to_all | solution.py:40
  174.7 0.0 copy-start.2
  174.7 0.1 reshape.78
  174.8 0.0 copy-start.1
  174.8 99.0 %all-to-all-done.1 = bf16[128,2,2,7168]{3,2,1,0:T(2,128)(2,1)} async-done(((bf16[128,2,2,7168]{3,2,1,0:T(2,128)(2,1)}), bf16[128,2,2,7168]{3,2,1,0:T(2,128)(2,1)}, u32[]{:S(2)}, u32[]{:S(2)}) %all-to-all-start.1) | async-done | bytes 7340064 | tf_op jit(solution)/shard_map/all_to_all | solution.py:40
  273.8 8.5 %bitcast_reduce_fusion = bf16[16,2,2,7168]{3,2,1,0:T(2,128)(2,1)S(1)} fusion(bf16[128,2,2,7168]{3,2,1,0:T(2,128)(2,1)} %all-to-all-done.1), kind=kLoop, calls=%fused_computation.10 | loop fusion | flops 3211264 | bytes 8257536 | tf_op jit(solution)/shard_map/reduce_sum | solution.py:44
  282.4 0.3 reshape.77
  282.7 0.8 gather_fusion
  283.6 0.0 copy-done.2
  283.6 1.0 multiply_reduce_fusion
  284.6 0.0 copy-done.1
  (4 shorter events, 0.1 us)
Async XLA Ops:
  0.0 3.2 %copy-start = (bf16[4,7168]{1,0:T(4,128)(2,1)S(1)}, bf16[4,7168]{1,0:T(4,128)(2,1)}, u32[]{:S(2)}) copy-start(bf16[4,7168]{1,0:T(4,128)(2,1)} %param.6) | copy-start | bytes 172036
  160.1 113.7 %all-to-all-start.1 = ((bf16[128,2,2,7168]{3,2,1,0:T(2,128)(2,1)}), bf16[128,2,2,7168]{3,2,1,0:T(2,128)(2,1)}, u32[]{:S(2)}, u32[]{:S(2)}) async-start(bf16[128,2,2,7168]{3,2,1,0:T(2,128)(2,1)} %copy.21), calls=%async_computation.1 | async-start | bytes 14680064 | tf_op jit(solution)/shard_map/all_to_all | solution.py:40
  174.7 108.9 %copy-start.2 = (f32[4,8]{1,0:T(4,128)S(1)}, f32[4,8]{1,0:T(4,128)}, u32[]{:S(2)}) copy-start(f32[4,8]{1,0:T(4,128)} %param.8) | copy-start | bytes 388
  174.8 109.8 %copy-start.1 = (bf16[4,7168]{1,0:T(4,128)(2,1)S(1)}, bf16[4,7168]{1,0:T(4,128)(2,1)}, u32[]{:S(2)}) copy-start(bf16[4,7168]{1,0:T(4,128)(2,1)} %param.6) | copy-start | bytes 172036
where the time goes:
time: 288 us; the launch traced here: 285 us
  blocking collectives  101 us (35%)
  waiting for transfers between devices  99 us (34%)
  local copies, waits for them, and re-layouts  39 us (14%)
  matrix products  18.6 us (6%)
  starting transfers between devices  14.6 us (5%)
  other arithmetic  11.9 us (4%)
    all_to_all x1, blocking collectives, body(): lax.all_to_all(copies, ('sect', 'grp', 'dev'), split_axis=0, concat_axis=...  101 us
    all_to_all x1, waiting for transfers between devices, body(): lax.all_to_all(flattened, ('sect', 'grp', 'dev'), split_axis=0, concat_ax...  99 us
    reshape x1, local copies, waits for them, and re-layouts, body(): partial_value.reshape(groups * lane_count, local_experts, CAP, model_width)  28.1 us
    all_to_all x1, starting transfers between devices, body(): lax.all_to_all(flattened, ('sect', 'grp', 'dev'), split_axis=0, concat_ax...  14.6 us
    reduce_sum x1, other arithmetic, body(): jnp.sum(returned.astype(jnp.float32), axis=1).astype(jnp.bfloat16)  8.55 us
    dot_general x1, matrix products, body(): jnp.einsum('jabcf,jfd->abjcd', hidden, w_down, preferred_element_type=jnp...  8.13 us
  transfers between devices with their start and end apart: 1, of which 1 were waited for; matrix products, arithmetic and copies ran while one was open for 0% of the time, Pallas kernels for 0%

commit v1 on v0

v1 whole, which is shorter than its diff:
```python
import functools

import jax
import jax.numpy as jnp
from jax import lax
from jax.experimental import pallas as pl
from jax.experimental.pallas import tpu as pltpu
from jax.sharding import PartitionSpec as P

ALL = ("sect", "grp", "dev")
MESH = pl.DeviceIdType.MESH
SIDE = 4
LANES = 128
ORDERS = ((0, 1, 2), (1, 2, 0), (2, 0, 1))


def thirds(width):
    tiles = width // LANES
    counts = [tiles // 3 + (1 if i < tiles % 3 else 0) for i in range(3)]
    parts, low = [], 0
    for count in counts:
        cut = low + (count + 1) // 2 * LANES
        high = low + count * LANES
        parts.append((low, cut, high))
        low = high
    return parts


def kernel(half, t8, wg_hbm, wu_hbm, wd_hbm, out, tr, xs, wall, wd, hid, ps, r0, *rest):
    fa, fb, rl, rr, fin = rest[0:9], rest[9:18], rest[18:27], rest[27:36], rest[36]
    wsem, ex_s, ex_r, ag_s, ag_r, dd_s, dd_r, pr_s, pr_r, rs_s, rs_r = rest[37:]
    wide = half + LANES
    experts = wg_hbm.shape[0]
    hidden_width = wg_hbm.shape[2]
    c, g, d = lax.axis_index("sect"), lax.axis_index("grp"), lax.axis_index("dev")
    other = 1 - c
    me = (g // 2, d % SIDE, (g % 2) * 2 + d // SIDE)

    def device(pos, core):
        x, y, z = pos
        return {"sect": core, "grp": x * 2 + z // 2, "dev": (z % 2) * SIDE + y}

    def shifted(axis, by):
        return tuple(lax.rem(m + by, SIDE) if a == axis else m for a, m in enumerate(me))

    twin = device(me, other)
    right = [device(shifted(a, 1), c) for a in range(3)]
    left = [device(shifted(a, SIDE - 1), c) for a in range(3)]

    barrier = pltpu.get_barrier_semaphore()
    for peer in [twin] + right + left:
        pl.semaphore_signal(barrier, inc=1, device_id=peer, device_id_type=MESH)

    weights = []
    for j in range(experts):
        for i, src in enumerate((wg_hbm, wu_hbm)):
            at = (2 * j + i) * hidden_width
            weights.append(
                pltpu.make_async_copy(src.at[j], wall.at[:, at : at + hidden_width], wsem.at[2 * j + i])
            )
    for j in range(experts):
        for h in range(2):
            weights.append(
                pltpu.make_async_copy(
                    wd_hbm.at[j, :, h * half : (h + 1) * half],
                    wd.at[h, j * hidden_width : (j + 1) * hidden_width],
                    wsem.at[2 * experts + 2 * j + h],
                )
            )
    for copy in weights:
        copy.start()
    pl.semaphore_wait(barrier, 7)

    def remote(src, dst, send, recv, peer):
        return pltpu.make_async_remote_copy(
            src_ref=src, dst_ref=dst, send_sem=send, recv_sem=recv, device_id=peer, device_id_type=MESH
        )

    def spot(part, stage, value):
        order = ORDERS[part]
        index = []
        for axis in range(3):
            if axis in order[:stage]:
                index.append(slice(None))
            elif axis == order[stage]:
                index.append(value)
            else:
                index.append(me[axis])
        return tuple(index) + (slice(None),)

    sent = []

    def go(copy):
        copy.start()
        sent.append(copy)

    swap = remote(t8.at[other], tr, ex_s, ex_r, twin)
    swap.start()
    swap.wait()
    xs[(c,) + me] = t8[c] + tr[...]

    ag_parts = thirds(wide)

    def ag(part, stage, kind, value, low, high, peer):
        ref = xs.at[(c,) + spot(part, stage, value) + (slice(low, high),)]
        return remote(ref, ref, ag_s.at[part, stage, kind], ag_r.at[part, stage, kind], peer)

    def across(part, stage, kind, half_index, value):
        low, _, high = ag_parts[part]
        ref = xs.at[(half_index,) + spot(part, stage, value) + (slice(low, high),)]
        return remote(ref, ref, dd_s.at[part, stage, kind], dd_r.at[part, stage, kind], twin)

    for stage in range(3):
        for part in range(3):
            axis = ORDERS[part][stage]
            low, cut, high = ag_parts[part]
            go(ag(part, stage, 0, me[axis], low, high, right[axis]))
            go(ag(part, stage, 1, me[axis], low, high, left[axis]))
            if stage == 0:
                go(across(part, stage, 3, c, me[axis]))
        for part in range(3):
            axis = ORDERS[part][stage]
            low, cut, high = ag_parts[part]
            before, after = shifted(axis, SIDE - 1)[axis], shifted(axis, 1)[axis]
            ag(part, stage, 0, before, low, high, twin).wait_recv()
            go(ag(part, stage, 2, before, low, cut, right[axis]))
            go(across(part, stage, 0, c, before))
            ag(part, stage, 1, after, low, high, twin).wait_recv()
            go(ag(part, stage, 3, after, cut, high, left[axis]))
            go(across(part, stage, 1, c, after))
        for part in range(3):
            axis = ORDERS[part][stage]
            low, cut, high = ag_parts[part]
            far = shifted(axis, 2)[axis]
            ag(part, stage, 2, far, low, cut, twin).wait_recv()
            ag(part, stage, 3, far, cut, high, twin).wait_recv()
            go(across(part, stage, 2, c, far))
    for stage in range(3):
        for part in range(3):
            axis = ORDERS[part][stage]
            for kind, by in ((3, 0), (0, SIDE - 1), (1, 1), (2, 2)):
                if kind < 3 or stage == 0:
                    across(part, stage, kind, other, shifted(axis, by)[axis]).wait_recv()
    for copy in weights:
        copy.wait()

    first = (c * 8 + g) * experts
    row = lax.broadcasted_iota(jnp.int32, (LANES, hidden_width), 0)
    picks = []
    for j in range(experts):
        e = first + j
        hit = (row == e) | (row == e + 32) | (row == e + 64)
        picks.append(jnp.where(hit, 1.0, 0.0).astype(jnp.bfloat16))

    span = 2
    rows = span * SIDE * SIDE * 8

    def up_step(m, carry):
        at = pl.ds(m * span, span)
        v0 = xs[0, at, :, :, :, 0:half].reshape(rows, half)
        v1 = xs[1, at, :, :, :, 0:half].reshape(rows, half)
        share = xs[0, at, :, :, :, half:wide].reshape(rows, LANES)
        for j in range(experts):
            cols = slice(2 * j * hidden_width, (2 * j + 2) * hidden_width)
            both = jnp.dot(v0, wall[0:half, cols], preferred_element_type=jnp.float32)
            both += jnp.dot(v1, wall[half : 2 * half, cols], preferred_element_type=jnp.float32)
            gate, up = both[:, :hidden_width], both[:, hidden_width:]
            weight = jnp.dot(share, picks[j], preferred_element_type=jnp.float32)
            act = gate / (1.0 + jnp.exp(-gate)) * up * weight
            hid[pl.ds(pl.multiple_of(m * rows, rows), rows), j * hidden_width : (j + 1) * hidden_width] = act.astype(
                jnp.bfloat16
            )
        return carry

    lax.fori_loop(0, SIDE // span, up_step, 0)

    rs_parts = thirds(half)

    def down(half_index, part):
        low, _, high = rs_parts[part]

        def step(m, carry):
            value = jnp.dot(
                hid[pl.ds(pl.multiple_of(m * rows, rows), rows), :],
                wd[half_index, :, low:high],
                preferred_element_type=jnp.float32,
            ).astype(jnp.bfloat16)
            ps[half_index, pl.ds(m * span, span), :, :, :, low:high] = value.reshape(
                span, SIDE, SIDE, 8, high - low
            )
            return carry

        lax.fori_loop(0, SIDE // span, step, 0)

    def pair(part, half_index):
        low, _, high = rs_parts[part]
        cols = (slice(None),) * 4 + (slice(low, high),)
        return remote(
            ps.at[(half_index,) + cols], r0.at[cols], pr_s.at[part], pr_r.at[part], twin
        )

    def plus(index, *others):
        total = ps[index].astype(jnp.float32)
        for value in others:
            total += value.astype(jnp.float32)
        ps[index] = total.astype(jnp.bfloat16)

    def rs(part, stage, kind, value, low, high, buf, peer):
        base = rs_parts[part][0]
        ref = ps.at[(c,) + spot(part, stage, value) + (slice(low, high),)]
        dst = buf[part * 3 + stage]
        dst = dst.at[(slice(None),) * (stage + 1) + (slice(low - base, high - base),)] if kind > 1 else dst
        return remote(ref, dst, rs_s.at[part, stage, kind], rs_r.at[part, stage, kind], peer)

    def copy_of(part, stage, kind):
        axis = ORDERS[part][stage]
        low, cut, high = rs_parts[part]
        far, after, before = (shifted(axis, by)[axis] for by in (2, 1, SIDE - 1))
        value, start, stop, buf, peer = (
            (far, low, cut, fa, right),
            (far, cut, high, fb, left),
            (after, cut, high, rl, right),
            (before, low, cut, rr, left),
            (after, low, cut, rl, right),
            (before, cut, high, rr, left),
        )[kind]
        return rs(part, stage, kind, value, start, stop, buf, peer[axis])

    def open_stage(part, stage):
        for kind in range(4):
            go(copy_of(part, stage, kind))

    for part in range(3):
        down(other, part)
        go(pair(part, other))
    for part in range(3):
        down(c, part)
        pair(part, c).wait_recv()
        low, _, high = rs_parts[part]

        def add_pair(i, carry):
            plus((c, i, slice(None), slice(None), slice(None), slice(low, high)), r0[i, :, :, :, low:high])
            return carry

        lax.fori_loop(0, SIDE, add_pair, 0)
        open_stage(part, 2)

    def accumulate(part, stage, value, low, high, others, base):
        index = (c,) + spot(part, stage, value) + (slice(low, high),)
        if stage < 2:
            tail = (slice(None),) * (stage + 1) + (slice(low - base, high - base),)
            plus(index, *[o[tail] for o in others])
        else:
            free = [i for i, s in enumerate(index[:-2]) if isinstance(s, slice)][0]

            def step(i, carry):
                inner = tuple(i if k == free else s for k, s in enumerate(index))
                plus(inner, *[o[i, :, :, low - base : high - base] for o in others])
                return carry

            lax.fori_loop(0, SIDE, step, 0)

    for stage in (2, 1, 0):
        for part in range(3):
            axis = ORDERS[part][stage]
            low, cut, high = rs_parts[part]
            after, before = shifted(axis, 1)[axis], shifted(axis, SIDE - 1)[axis]
            k = part * 3 + stage
            copy_of(part, stage, 0).wait_recv()
            accumulate(part, stage, after, low, cut, [fa[k]], low)
            go(copy_of(part, stage, 4))
            copy_of(part, stage, 1).wait_recv()
            accumulate(part, stage, before, cut, high, [fb[k]], cut)
            go(copy_of(part, stage, 5))
        for part in range(3):
            axis = ORDERS[part][stage]
            low, cut, high = rs_parts[part]
            k = part * 3 + stage
            for kind in range(2, 6):
                copy_of(part, stage, kind).wait_recv()
            accumulate(part, stage, me[axis], low, high, [rl[k], rr[k]], low)
            if stage:
                open_stage(part, stage - 1)

    back = remote(ps.at[(c,) + me], fin, ex_s, ex_r, twin)
    back.start()
    out[c] = ps[(c,) + me]
    back.wait()
    out[other] = fin[...]
    for copy in sent:
        copy.wait_send()


def body(tokens, expert_ids, gate_weights, w_gate, w_up, w_down):
    row_count, model_width = tokens.shape
    half = model_width // 2
    experts, _, hidden_width = w_gate.shape
    c = lax.axis_index("sect")
    catalog = jnp.arange(32, dtype=jnp.int32)
    naming = expert_ids[:, :, None] == catalog[None, None, :]
    share = jnp.sum(jnp.where(naming, gate_weights[:, :, None], 0.0), axis=1)
    high = lax.reduce_precision(share, 8, 7)
    middle = lax.reduce_precision(share - high, 8, 7)
    low = share - high - middle
    extra = jnp.concatenate([high, middle, low, jnp.zeros_like(low)], axis=1).astype(jnp.bfloat16)
    mine = jnp.stack([jnp.concatenate([tokens[:, h * half : (h + 1) * half], extra], axis=1) for h in range(2)])
    spread = jnp.concatenate([mine, mine], axis=1)
    owner = lax.broadcasted_iota(jnp.int32, spread.shape, 1) // row_count
    t8 = jnp.where(owner == c, spread, jnp.zeros_like(spread))

    wide = half + LANES
    sides = (SIDE,) * 3
    bf16 = jnp.bfloat16
    rs_parts = thirds(half)
    lead = [(SIDE,) * s + (8,) for s in range(3)]
    sizes = {
        "fa": [lead[s] + (cut - lo,) for lo, cut, hi in rs_parts for s in range(3)],
        "fb": [lead[s] + (hi - cut,) for lo, cut, hi in rs_parts for s in range(3)],
        "rl": [lead[s] + (hi - lo,) for lo, cut, hi in rs_parts for s in range(3)],
    }
    scratch = [
        pltpu.VMEM((8, wide), bf16),
        pltpu.VMEM((2,) + sides + (8, wide), bf16),
        pltpu.VMEM((model_width, 2 * experts * hidden_width), bf16),
        pltpu.VMEM((2, experts * hidden_width, half), bf16),
        pltpu.VMEM((8 * SIDE**3, experts * hidden_width), bf16),
        pltpu.VMEM((2,) + sides + (8, half), bf16),
        pltpu.VMEM(sides + (8, half), bf16),
    ]
    scratch += [pltpu.VMEM(s, bf16) for key in ("fa", "fb", "rl", "rl") for s in sizes[key]]
    scratch += [pltpu.VMEM((8, half), bf16)]
    dma = pltpu.SemaphoreType.DMA
    scratch += [
        dma((4 * experts,)),
        dma,
        dma,
        dma((3, 3, 4)),
        dma((3, 3, 4)),
        dma((3, 3, 4)),
        dma((3, 3, 4)),
        dma((3,)),
        dma((3,)),
        dma((3, 3, 6)),
        dma((3, 3, 6)),
    ]
    anywhere = pl.BlockSpec(memory_space=pl.ANY)
    vmem = pl.BlockSpec(memory_space=pltpu.VMEM)
    out = pl.pallas_call(
        functools.partial(kernel, half),
        out_shape=jax.ShapeDtypeStruct((2, 8, half), bf16),
        in_specs=[vmem, anywhere, anywhere, anywhere],
        out_specs=vmem,
        scratch_shapes=scratch,
        compiler_params=pltpu.CompilerParams(
            collective_id=0, has_side_effects=True, vmem_limit_bytes=60 * 1024 * 1024
        ),
    )(t8, w_gate, w_up, w_down)
    picked = lax.dynamic_slice_in_dim(out, c * row_count, row_count, axis=1)
    return jnp.concatenate([picked[0], picked[1]], axis=1)


def solution(mesh):
    in_specs = (
        P(ALL, None),
        P(ALL, None),
        P(ALL, None),
        P(("sect", "grp"), None, "dev"),
        P(("sect", "grp"), None, "dev"),
        P(("sect", "grp"), "dev", None),
    )
    return jax.shard_map(body, mesh=mesh, in_specs=in_specs, out_specs=P(ALL, None), check_vma=False)
```

time: 288 us -> 88.8 us (0.31); the launches traced: 285 us -> 88.5 us
  blocking collectives: 101 us -> 0 us
  waiting for transfers between devices: 99 us -> 0 us
  Pallas kernels: 0 us -> 84.5 us
  local copies, waits for them, and re-layouts: 39 us -> 1.87 us
  matrix products: 18.6 us -> 0 us
  starting transfers between devices: 14.6 us -> 0 us
  other arithmetic: 11.9 us -> 2.18 us
    all_to_all x1 -> x0, blocking collectives: 101 us -> none  [body(): lax.all_to_all(copies, ('sect', 'grp', 'dev'), split_axis=0, concat_axis=...]
    all_to_all x1 -> x0, waiting for transfers between devices: 99 us -> none  [body(): lax.all_to_all(flattened, ('sect', 'grp', 'dev'), split_axis=0, concat_ax...]
    pallas_call x0 -> x1, Pallas kernels: none -> 84.5 us  [body(): pl.pallas_call(functools.partial(kernel, half), out_shape=jax.ShapeDtypeS...]
    reshape x3 -> x0, local copies, waits for them, and re-layouts: 28.5 us -> none  [the longest x1 28.1 us: body(): partial_value.reshape(groups * lane_count, local_experts, CAP, model_width)]
    dot_general x4 -> x0, matrix products: 18.6 us -> none  [the longest x1 8.13 us: body(): jnp.einsum('jabcf,jfd->abjcd', hidden, w_down, preferred_element_type=jnp...]
    all_to_all x1 -> x0, starting transfers between devices: 14.6 us -> none  [body(): lax.all_to_all(flattened, ('sect', 'grp', 'dev'), split_axis=0, concat_ax...]
    reduce_sum x4 -> x1, other arithmetic: 10.4 us -> 0.78 us  [body(): share = jnp.sum(jnp.where(naming, gate_weights[:, :, None], 0.0), axis=1)]
    broadcast_in_dim x2 -> x1, local copies, waits for them, and re-layouts: 5.04 us -> 0.01 us  [body(): jnp.zeros_like(low)]
  transfers between devices with their start and end apart: 1 -> 0, of which waited for: 1 -> 0; matrix products, arithmetic and copies ran while one was open for 0% -> 0% of each run, Pallas kernels for 0% -> 0%
where the time goes in v1:
time: 88.8 us; the launch traced here: 88.5 us
  Pallas kernels  84.5 us (95%)
  other arithmetic  2.18 us (2%)
  local copies, waits for them, and re-layouts  1.87 us (2%)
    pallas_call x1, Pallas kernels, body(): pl.pallas_call(functools.partial(kernel, half), out_shape=jax.ShapeDtypeS...  84.5 us

profile of v1, /device:TPU:1, one launch (start us, length us, event | category | flops | bytes accessed | tf_op | source)
XLA Modules:
  0.0 88.5 jit_solution(6163263216307295225)
XLA Ops:
  0.0 0.8 select_reduce_fusion
  0.8 0.8 fusion.2
  1.6 0.1 concatenate.16
  1.7 0.1 concatenate.17
  1.8 0.7 fusion.t8
  2.5 84.5 %shard_map.64 = bf16[2,8,3584]{2,1,0:T(8,128)(2,1)} custom-call(bf16[2,8,3712]{2,1,0:T(8,128)(2,1)} %fusion.t8, bf16[2,7168,256]{2,1,0:T(8,128)(2,1)} %wg_hbm.1, bf16[2,7168,256]{2,1,0:T(8,128)(2,1)} %wu_hbm.1, bf16[2,256,7168]{2,1,0:T(8,128)(2,1)} %wd_hbm.1), custom_call_target="tpu_custom_call" | custom-call | tf_op jit(solution)/shard_map/pallas_call | solution.py:348
  87.0 0.9 dynamic-slice_bitcast_fusion.1
  87.9 0.7 pad_maximum_fusion
  (4 shorter events, 0.0 us)

commit v2 on v1

v2 whole, which is shorter than its diff:
```python
import functools

import jax
import jax.numpy as jnp
from jax import lax
from jax.experimental import pallas as pl
from jax.experimental.pallas import tpu as pltpu
from jax.sharding import PartitionSpec as P

ALL = ("sect", "grp", "dev")
MESH = pl.DeviceIdType.MESH
SIDE = 4
LANES = 128
ORDERS = ((0, 1, 2), (1, 2, 0), (2, 0, 1))


def thirds(width):
    tiles = width // LANES
    counts = [tiles // 3 + (1 if i < tiles % 3 else 0) for i in range(3)]
    parts, low = [], 0
    for count in counts:
        cut = low + (count + 1) // 2 * LANES
        high = low + count * LANES
        parts.append((low, cut, high))
        low = high
    return parts


def kernel(half, t8, wg_hbm, wu_hbm, wd_hbm, out, tr, xs, wall, wd, acc, hid, ps, r0, *rest):
    fa, fb, rl, rr, s1, s0 = (rest[i : i + 3] for i in range(0, 18, 3))
    fin = rest[18]
    wsem, ex_s, ex_r, ag_s, ag_r, dd_s, dd_r, pr_s, pr_r, rs_s, rs_r = rest[19:]
    wide = half + LANES
    experts = wg_hbm.shape[0]
    hidden_width = wg_hbm.shape[2]
    c, g, d = lax.axis_index("sect"), lax.axis_index("grp"), lax.axis_index("dev")
    other = 1 - c
    me = (g // 2, d % SIDE, (g % 2) * 2 + d // SIDE)

    def device(pos, core):
        x, y, z = pos
        return {"sect": core, "grp": x * 2 + z // 2, "dev": (z % 2) * SIDE + y}

    def shifted(axis, by):
        return tuple(lax.rem(m + by, SIDE) if a == axis else m for a, m in enumerate(me))

    twin = device(me, other)
    right = [device(shifted(a, 1), c) for a in range(3)]
    left = [device(shifted(a, SIDE - 1), c) for a in range(3)]
    far = [device(shifted(a, 2), c) for a in range(3)]
    toward = {1: right, 2: far, 3: left}

    barrier = pltpu.get_barrier_semaphore()
    for peer in [twin] + right + left + far:
        pl.semaphore_signal(barrier, inc=1, device_id=peer, device_id_type=MESH)

    weights = []
    for j in range(experts):
        for i, src in enumerate((wg_hbm, wu_hbm)):
            at = (2 * j + i) * hidden_width
            for h in range(2):
              weights.append(
                pltpu.make_async_copy(src.at[j, h * half : (h + 1) * half], wall.at[h, :, at : at + hidden_width], wsem.at[h, 2 * j + i])
            )
    for j in range(experts):
        for h in range(2):
            weights.append(
                pltpu.make_async_copy(
                    wd_hbm.at[j, :, h * half : (h + 1) * half],
                    wd.at[h, j * hidden_width : (j + 1) * hidden_width],
                    wsem.at[h, 2 * experts + j],
                )
            )
    for copy in weights:
        copy.start()
    pl.semaphore_wait(barrier, 10)

    def remote(src, dst, send, recv, peer):
        return pltpu.make_async_remote_copy(
            src_ref=src, dst_ref=dst, send_sem=send, recv_sem=recv, device_id=peer, device_id_type=MESH
        )

    def spot(part, stage, value):
        order = ORDERS[part]
        index = []
        for axis in range(3):
            if axis in order[:stage]:
                index.append(slice(None))
            elif axis == order[stage]:
                index.append(value)
            else:
                index.append(me[axis])
        return tuple(index) + (slice(None),)

    sent = []

    def go(copy):
        copy.start()
        sent.append(copy)

    swap = remote(t8.at[other], tr, ex_s, ex_r, twin)
    swap.start()
    swap.wait()
    xs[(c,) + me] = t8[c] + tr[...]

    ag_parts = thirds(wide)
    steps = (1, SIDE - 1, 2)

    def block(core_half, part, stage, value):
        low, _, high = ag_parts[part]
        return xs.at[(core_half,) + spot(part, stage, value) + (slice(low, high),)]

    def line(core_half, part, second, third):
        low, _, high = ag_parts[part]
        index = [slice(None)] * 3
        index[ORDERS[part][1]] = second
        index[ORDERS[part][2]] = third
        return xs.at[(core_half,) + tuple(index) + (slice(None), slice(low, high))]

    def coord(part, stage, by):
        axis = ORDERS[part][stage]
        return shifted(axis, by)[axis]

    def ag(part, slot, ref, peer):
        return remote(ref, ref, ag_s.at[part, slot], ag_r.at[part, slot], peer)

    def across(part, slot, ref):
        return remote(ref, ref, dd_s.at[part, slot], dd_r.at[part, slot], twin)

    def send_line(part, row, second):
        ref = line(c, part, second, coord(part, 2, 0))
        for k, by in enumerate(steps):
            go(ag(part, 6 + 4 * k + row, ref, toward[by][ORDERS[part][2]]))
        go(across(part, row, ref))

    for part in range(3):
        ref = block(c, part, 0, coord(part, 0, 0))
        for k, by in enumerate(steps):
            go(ag(part, k, ref, toward[by][ORDERS[part][0]]))
    acc[...] = jnp.zeros_like(acc)
    for part in range(3):
        for k, by in enumerate(steps):
            ag(part, k, block(c, part, 0, coord(part, 0, SIDE - by)), twin).wait_recv()
        ref = line(c, part, coord(part, 1, 0), coord(part, 2, 0))
        for k, by in enumerate(steps):
            go(ag(part, 3 + k, ref, toward[by][ORDERS[part][1]]))
        send_line(part, 0, coord(part, 1, 0))
    for k, by in enumerate(steps):
        for part in range(3):
            second = coord(part, 1, SIDE - by)
            ag(part, 3 + k, line(c, part, second, coord(part, 2, 0)), twin).wait_recv()
            send_line(part, 1 + k, second)

    def piece(core_half, part, third):
        low, _, high = ag_parts[part]
        high = min(high, half)
        at = spot(part, 2, third)
        value = xs[(core_half,) + at + (slice(low, high),)].reshape(SIDE * SIDE * 8, high - low)
        got = jnp.dot(value, wall[core_half, low:high, :], preferred_element_type=jnp.float32)
        acc[at + (slice(None),)] += got.reshape(SIDE, SIDE, 8, acc.shape[-1])

    for copy in weights:
        copy.wait()
    for part in range(3):
        piece(c, part, coord(part, 2, 0))
    for part in range(3):
        for row, by in enumerate((0,) + steps):
            across(part, row, line(other, part, coord(part, 1, SIDE - by), coord(part, 2, 0))).wait_recv()
        piece(other, part, coord(part, 2, 0))
    for k, by in enumerate(steps):
        for part in range(3):
            third = coord(part, 2, SIDE - by)
            for row, back_by in enumerate((0,) + steps):
                ag(part, 6 + 4 * k + row, line(c, part, coord(part, 1, SIDE - back_by), third), twin).wait_recv()
            go(across(part, 4 + k, block(c, part, 2, third)))
            piece(c, part, third)
        for part in range(3):
            third = coord(part, 2, SIDE - by)
            across(part, 4 + k, block(other, part, 2, third)).wait_recv()
            piece(other, part, third)

    first = (c * 8 + g) * experts
    row = lax.broadcasted_iota(jnp.int32, (LANES, hidden_width), 0)
    picks = []
    for j in range(experts):
        e = first + j
        hit = (row == e) | (row == e + 32) | (row == e + 64)
        picks.append(jnp.where(hit, 1.0, 0.0).astype(jnp.bfloat16))
    slab = SIDE * SIDE * 8

    def act_step(i, carry):
        share = xs[0, i, :, :, :, half:wide].reshape(slab, LANES)
        for j in range(experts):
            at = 2 * j * hidden_width
            gate = acc[i, :, :, :, at : at + hidden_width].reshape(slab, hidden_width)
            up = acc[i, :, :, :, at + hidden_width : at + 2 * hidden_width].reshape(slab, hidden_width)
            weight = jnp.dot(share, picks[j], preferred_element_type=jnp.float32)
            act = gate / (1.0 + jnp.exp(-gate)) * up * weight
            hid[pl.ds(pl.multiple_of(i * slab, slab), slab), j * hidden_width : (j + 1) * hidden_width] = act.astype(
                jnp.bfloat16
            )
        return carry

    lax.fori_loop(0, SIDE, act_step, 0)
    span = 2
    rows = span * slab

    rs_parts = thirds(half)

    def bounds(part, sub):
        low, cut, high = rs_parts[part]
        return (low, cut) if sub == 0 else (cut, high)

    def down(half_index, part, sub):
        low, high = bounds(part, sub)

        def step(m, carry):
            value = jnp.dot(
                hid[pl.ds(pl.multiple_of(m * rows, rows), rows), :],
                wd[half_index, :, low:high],
                preferred_element_type=jnp.float32,
            ).astype(jnp.bfloat16)
            ps[half_index, pl.ds(m * span, span), :, :, :, low:high] = value.reshape(
                span, SIDE, SIDE, 8, high - low
            )
            return carry

        lax.fori_loop(0, SIDE // span, step, 0)

    def pair(half_index, part, sub):
        low, high = bounds(part, sub)
        cols = (slice(None),) * 4 + (slice(low, high),)
        return remote(
            ps.at[(half_index,) + cols], r0.at[cols], pr_s.at[part, sub], pr_r.at[part, sub], twin
        )

    def plus(index, *others):
        total = ps[index].astype(jnp.float32)
        for value in others:
            total += value.astype(jnp.float32)
        ps[index] = total.astype(jnp.bfloat16)

    def add_pair(part, sub):
        low, high = bounds(part, sub)

        def step(i, carry):
            plus((c, i, slice(None), slice(None), slice(None), slice(low, high)), r0[i, :, :, :, low:high])
            return carry

        lax.fori_loop(0, SIDE, step, 0)

    def big(part, kind):
        axis = ORDERS[part][2]
        low, cut, high = rs_parts[part]
        by, start, stop, buf, peer = (
            (2, low, cut, fa, right),
            (2, cut, high, fb, left),
            (1, cut, high, rl, right),
            (SIDE - 1, low, cut, rr, left),
            (1, low, cut, rl, right),
            (SIDE - 1, cut, high, rr, left),
        )[kind]
        ref = ps.at[(c,) + spot(part, 2, shifted(axis, by)[axis]) + (slice(start, stop),)]
        dst = buf[part]
        if kind > 1:
            dst = dst.at[:, :, :, start - low : stop - low]
        return remote(ref, dst, rs_s.at[part, kind], rs_r.at[part, kind], peer[axis])

    def small(part, stage, k):
        axis = ORDERS[part][stage]
        low, _, high = rs_parts[part]
        ref = ps.at[(c,) + spot(part, stage, shifted(axis, steps[k])[axis]) + (slice(low, high),)]
        dst = (s0, s1)[stage][part].at[k]
        return remote(
            ref, dst, rs_s.at[part, 6 + 3 * stage + k], rs_r.at[part, 6 + 3 * stage + k], toward[steps[k]][axis]
        )

    def accumulate(part, by, low, high, others):
        axis = ORDERS[part][2]
        base = rs_parts[part][0]
        index = (c,) + spot(part, 2, shifted(axis, by)[axis]) + (slice(low, high),)
        free = [i for i, s in enumerate(index[:-2]) if isinstance(s, slice)][0]

        def step(i, carry):
            inner = tuple(i if k == free else s for k, s in enumerate(index))
            plus(inner, *[o[i, :, :, at : at + high - low] for o, at in others])
            return carry

        lax.fori_loop(0, SIDE, step, 0)

    queue = [(part, sub) for sub in range(2) for part in range(3)]
    down(other, *queue[0])
    go(pair(other, *queue[0]))
    for i, (part, sub) in enumerate(queue):
        if i + 1 < len(queue):
            down(other, *queue[i + 1])
            go(pair(other, *queue[i + 1]))
        down(c, part, sub)
        pair(c, part, sub).wait_recv()
        add_pair(part, sub)
        for kind in ((0, 3), (1, 2))[sub]:
            go(big(part, kind))
    for part in range(3):
        low, cut, high = rs_parts[part]
        big(part, 0).wait_recv()
        accumulate(part, 1, low, cut, [(fa[part], 0)])
        go(big(part, 4))
    for part in range(3):
        low, cut, high = rs_parts[part]
        big(part, 1).wait_recv()
        accumulate(part, SIDE - 1, cut, high, [(fb[part], 0)])
        go(big(part, 5))
    for part in range(3):
        low, cut, high = rs_parts[part]
        for kind in range(2, 6):
            big(part, kind).wait_recv()
        accumulate(part, 0, low, high, [(rl[part], 0), (rr[part], 0)])
        for k in range(3):
            go(small(part, 1, k))
    for stage in (1, 0):
        for part in range(3):
            low, cut, high = rs_parts[part]
            for k in range(3):
                small(part, stage, k).wait_recv()
            index = (c,) + spot(part, stage, me[ORDERS[part][stage]]) + (slice(low, high),)
            plus(index, *[(s0, s1)[stage][part][k] for k in range(3)])
            if stage:
                for k in range(3):
                    go(small(part, 0, k))

    back = remote(ps.at[(c,) + me], fin, ex_s, ex_r, twin)
    back.start()
    out[c] = ps[(c,) + me]
    back.wait()
    out[other] = fin[...]
    for copy in sent:
        copy.wait_send()


def body(tokens, expert_ids, gate_weights, w_gate, w_up, w_down):
    row_count, model_width = tokens.shape
    half = model_width // 2
    experts, _, hidden_width = w_gate.shape
    c = lax.axis_index("sect")
    catalog = jnp.arange(32, dtype=jnp.int32)
    naming = expert_ids[:, :, None] == catalog[None, None, :]
    share = jnp.sum(jnp.where(naming, gate_weights[:, :, None], 0.0), axis=1)
    high = lax.reduce_precision(share, 8, 7)
    middle = lax.reduce_precision(share - high, 8, 7)
    low = share - high - middle
    extra = jnp.concatenate([high, middle, low, jnp.zeros_like(low)], axis=1).astype(jnp.bfloat16)
    mine = jnp.stack([jnp.concatenate([tokens[:, h * half : (h + 1) * half], extra], axis=1) for h in range(2)])
    spread = jnp.concatenate([mine, mine], axis=1)
    owner = lax.broadcasted_iota(jnp.int32, spread.shape, 1) // row_count
    t8 = jnp.where(owner == c, spread, jnp.zeros_like(spread))

    wide = half + LANES
    sides = (SIDE,) * 3
    bf16 = jnp.bfloat16
    rs_parts = thirds(half)
    plane = (SIDE, SIDE, 8)
    landing = [plane + (cut - lo,) for lo, cut, hi in rs_parts]
    landing += [plane + (hi - cut,) for lo, cut, hi in rs_parts]
    landing += [plane + (hi - lo,) for lo, cut, hi in rs_parts] * 2
    landing += [(3, SIDE, 8, hi - lo) for lo, cut, hi in rs_parts]
    landing += [(3, 8, hi - lo) for lo, cut, hi in rs_parts]
    scratch = [
        pltpu.VMEM((8, wide), bf16),
        pltpu.VMEM((2,) + sides + (8, wide), bf16),
        pltpu.VMEM((2, half, 2 * experts * hidden_width), bf16),
        pltpu.VMEM((2, experts * hidden_width, half), bf16),
        pltpu.VMEM(sides + (8, 2 * experts * hidden_width), jnp.float32),
        pltpu.VMEM((8 * SIDE**3, experts * hidden_width), bf16),
        pltpu.VMEM((2,) + sides + (8, half), bf16),
        pltpu.VMEM(sides + (8, half), bf16),
    ]
    scratch += [pltpu.VMEM(s, bf16) for s in landing]
    scratch += [pltpu.VMEM((8, half), bf16)]
    dma = pltpu.SemaphoreType.DMA
    scratch += [
        dma((2, 3 * experts)),
        dma,
        dma,
        dma((3, 18)),
        dma((3, 18)),
        dma((3, 7)),
        dma((3, 7)),
        dma((3, 2)),
        dma((3, 2)),
        dma((3, 12)),
        dma((3, 12)),
    ]
    anywhere = pl.BlockSpec(memory_space=pl.ANY)
    vmem = pl.BlockSpec(memory_space=pltpu.VMEM)
    out = pl.pallas_call(
        functools.partial(kernel, half),
        out_shape=jax.ShapeDtypeStruct((2, 8, half), bf16),
        in_specs=[vmem, anywhere, anywhere, anywhere],
        out_specs=vmem,
        scratch_shapes=scratch,
        compiler_params=pltpu.CompilerParams(
            collective_id=0, has_side_effects=True, vmem_limit_bytes=60 * 1024 * 1024
        ),
    )(t8, w_gate, w_up, w_down)
    picked = lax.dynamic_slice_in_dim(out, c * row_count, row_count, axis=1)
    return jnp.concatenate([picked[0], picked[1]], axis=1)


def solution(mesh):
    in_specs = (
        P(ALL, None),
        P(ALL, None),
        P(ALL, None),
        P(("sect", "grp"), None, "dev"),
        P(("sect", "grp"), None, "dev"),
        P(("sect", "grp"), "dev", None),
    )
    return jax.shard_map(body, mesh=mesh, in_specs=in_specs, out_specs=P(ALL, None), check_vma=False)
```

time: 88.8 us -> 80 us (0.901)
  Pallas kernels: 84.5 us -> 75.7 us
    pallas_call x1, Pallas kernels: 84.5 us -> 75.7 us  [body(): pl.pallas_call(functools.partial(kernel, half), out_shape=jax.ShapeDtypeS...]
where the time goes in v2:
time: 80 us; the launch traced here: 79.7 us
  Pallas kernels  75.7 us (95%)
  other arithmetic  2.18 us (3%)
  local copies, waits for them, and re-layouts  1.87 us (2%)
    pallas_call x1, Pallas kernels, body(): pl.pallas_call(functools.partial(kernel, half), out_shape=jax.ShapeDtypeS...  75.7 us

profile of v2, /device:TPU:1, one launch (start us, length us, event | category | flops | bytes accessed | tf_op | source)
XLA Modules:
  0.0 79.7 jit_solution(11705780768403371947)
XLA Ops:
  0.0 0.8 select_reduce_fusion
  0.8 0.8 fusion.2
  1.6 0.1 concatenate.16
  1.7 0.1 concatenate.17
  1.8 0.7 fusion.t8
  2.5 75.7 %shard_map.64 = bf16[2,8,3584]{2,1,0:T(8,128)(2,1)} custom-call(bf16[2,8,3712]{2,1,0:T(8,128)(2,1)} %fusion.t8, bf16[2,7168,256]{2,1,0:T(8,128)(2,1)} %wg_hbm.1, bf16[2,7168,256]{2,1,0:T(8,128)(2,1)} %wu_hbm.1, bf16[2,256,7168]{2,1,0:T(8,128)(2,1)} %wd_hbm.1), custom_call_target="tpu_custom_call" | custom-call | tf_op jit(solution)/shard_map/pallas_call | solution.py:395
  78.2 0.9 %dynamic-slice_bitcast_fusion.1 = (bf16[4,3584]{1,0:T(4,128)(2,1)S(1)}, bf16[4,3584]{1,0:T(4,128)(2,1)S(1)}) fusion(bf16[2,8,3584]{2,1,0:T(8,128)(2,1)} %shard_map.64, s32[]{:T(128)S(6)} %select_n.19, s32[]{:T(128)S(6)} %add.6), kind=kLoop, calls=%fused_computation.4 | loop fusion | bytes 114696 | tf_op jit(solution)/shard_map/squeeze | solution.py:406
  79.1 0.7 pad_maximum_fusion
  (4 shorter events, 0.0 us)

commit v3 on v2

v3 whole, which is shorter than its diff:
```python
import functools

import jax
import jax.numpy as jnp
from jax import lax
from jax.experimental import pallas as pl
from jax.experimental.pallas import tpu as pltpu
from jax.sharding import PartitionSpec as P

ALL = ("sect", "grp", "dev")
MESH = pl.DeviceIdType.MESH
SIDE = 4
LANES = 128
TILE = 256
ORDERS = ((0, 1, 2), (1, 2, 0), (2, 0, 1)) * 2


GATHER = (6, 6, 4, 4, 4, 5)
SCATTER = (6, 6, 4, 4, 4, 4)


def split(counts):
    parts, low = [], 0
    for count in counts:
        cut = low + (count + 1) // 2 * LANES
        high = low + count * LANES
        parts.append((low, cut, high))
        low = high
    return parts


def kernel(half, tokens, ids, shares, wg_hbm, wu_hbm, wd_hbm, out, t8, tr, xs, wall, wd, acc, hid, ps, r0, *rest):
    fa, fb, rl, rr, s1, s0 = (rest[i : i + 6] for i in range(0, 36, 6))
    fin = rest[36]
    wsem, ex_s, ex_r, ag_s, ag_r, dd_s, dd_r, pr_s, pr_r, rs_s, rs_r = rest[37:]
    wide = half + LANES
    experts = wg_hbm.shape[0]
    hidden_width = wg_hbm.shape[2]
    c, g, d = lax.axis_index("sect"), lax.axis_index("grp"), lax.axis_index("dev")
    other = 1 - c
    me = (g // 2, d % SIDE, (g % 2) * 2 + d // SIDE)

    def device(pos, core):
        x, y, z = pos
        return {"sect": core, "grp": x * 2 + z // 2, "dev": (z % 2) * SIDE + y}

    def shifted(axis, by):
        return tuple(lax.rem(m + by, SIDE) if a == axis else m for a, m in enumerate(me))

    twin = device(me, other)
    right = [device(shifted(a, 1), c) for a in range(3)]
    left = [device(shifted(a, SIDE - 1), c) for a in range(3)]
    far = [device(shifted(a, 2), c) for a in range(3)]
    toward = {1: right, 2: far, 3: left}

    barrier = pltpu.get_barrier_semaphore()
    for peer in [twin] + right + left + far:
        pl.semaphore_signal(barrier, inc=1, device_id=peer, device_id_type=MESH)

    weights = []
    for j in range(experts):
        for i, src in enumerate((wg_hbm, wu_hbm)):
            at = (2 * j + i) * hidden_width
            for h in range(2):
              weights.append(
                pltpu.make_async_copy(src.at[j, h * half : (h + 1) * half], wall.at[h, :, at : at + hidden_width], wsem.at[h, 2 * j + i])
            )
    for j in range(experts):
        for h in range(2):
            weights.append(
                pltpu.make_async_copy(
                    wd_hbm.at[j, :, h * half : (h + 1) * half],
                    wd.at[h, j * hidden_width : (j + 1) * hidden_width],
                    wsem.at[h, 2 * experts + j],
                )
            )
    for copy in weights:
        copy.start()
    lane = lax.broadcasted_iota(jnp.int32, (4, LANES), 1)
    share = jnp.zeros((4, LANES), jnp.float32)
    for k in range(ids.shape[1]):
        share += jnp.where((lane & 31) == ids[:, k : k + 1], shares[:, k : k + 1], 0.0)
    upper = share.astype(jnp.bfloat16).astype(jnp.float32)
    middle = (share - upper).astype(jnp.bfloat16).astype(jnp.float32)
    lower = share - upper - middle
    extra = jnp.where(lane < 32, upper, jnp.where(lane < 64, middle, jnp.where(lane < 96, lower, 0.0)))
    for h in range(2):
        for low, high, value in (
            (0, half, tokens[:, h * half : (h + 1) * half].astype(jnp.float32)),
            (half, wide, extra),
        ):
            eight = jnp.concatenate([value, value], axis=0)
            owner = lax.broadcasted_iota(jnp.int32, eight.shape, 0) // 4
            t8[h, :, low:high] = jnp.where(owner == c, eight, 0.0).astype(jnp.bfloat16)
    pl.semaphore_wait(barrier, 10)

    def remote(src, dst, send, recv, peer):
        return pltpu.make_async_remote_copy(
            src_ref=src, dst_ref=dst, send_sem=send, recv_sem=recv, device_id=peer, device_id_type=MESH
        )

    def spot(part, stage, value):
        order = ORDERS[part]
        index = []
        for axis in range(3):
            if axis in order[:stage]:
                index.append(slice(None))
            elif axis == order[stage]:
                index.append(value)
            else:
                index.append(me[axis])
        return tuple(index) + (slice(None),)

    sent = []

    def go(copy):
        copy.start()
        sent.append(copy)

    swap = remote(t8.at[other], tr, ex_s, ex_r, twin)
    swap.start()
    swap.wait()
    xs[(c,) + me] = t8[c] + tr[...]

    slab = SIDE * SIDE * 8
    ag_parts = split(GATHER)
    steps = (1, SIDE - 1, 2)

    def block(core_half, part, stage, value):
        low, _, high = ag_parts[part]
        return xs.at[(core_half,) + spot(part, stage, value) + (slice(low, high),)]

    def line(core_half, part, second, third):
        low, _, high = ag_parts[part]
        index = [slice(None)] * 3
        index[ORDERS[part][1]] = second
        index[ORDERS[part][2]] = third
        return xs.at[(core_half,) + tuple(index) + (slice(None), slice(low, high))]

    def coord(part, stage, by):
        axis = ORDERS[part][stage]
        return shifted(axis, by)[axis]

    def ag(part, slot, ref, peer):
        return remote(ref, ref, ag_s.at[part, slot], ag_r.at[part, slot], peer)

    def across(part, slot, ref):
        return remote(ref, ref, dd_s.at[part, slot], dd_r.at[part, slot], twin)

    def halved(part, sub, third):
        low, cut, high = ag_parts[part]
        cols = slice(low, cut) if sub == 0 else slice(cut, high)
        return xs.at[(c,) + spot(part, 2, third) + (cols,)]

    def pieces(core_half, part, *thirds):
        low, _, high = ag_parts[part]
        high = min(high, half)
        spots = [spot(part, 2, third) for third in thirds]
        values = [xs[(core_half,) + at + (slice(low, high),)].reshape(slab, high - low) for at in spots]
        value = values[0] if len(values) == 1 else jnp.concatenate(values, axis=0)
        for start in range(0, acc.shape[-1], TILE):
            got = jnp.dot(value, wall[core_half, low:high, start : start + TILE], preferred_element_type=jnp.float32)
            for i, at in enumerate(spots):
                mine = got[i * slab : (i + 1) * slab].reshape(SIDE, SIDE, 8, TILE)
                acc[at + (slice(start, start + TILE),)] += mine

    def first_hop(part):
        ref = block(c, part, 0, coord(part, 0, 0))
        for k, by in enumerate(steps):
            go(ag(part, k, ref, toward[by][ORDERS[part][0]]))

    def second_hop(part):
        for k, by in enumerate(steps):
            ag(part, k, block(c, part, 0, coord(part, 0, SIDE - by)), twin).wait_recv()
        ref = line(c, part, coord(part, 1, 0), coord(part, 2, 0))
        for k, by in enumerate(steps):
            go(ag(part, 3 + k, ref, toward[by][ORDERS[part][1]]))

    def third_hop(part, row):
        by = (0,) + steps
        ref = line(c, part, coord(part, 1, SIDE - by[row]), coord(part, 2, 0))
        if row:
            ag(part, 2 + row, ref, twin).wait_recv()
        go(ag(part, 6 + row, ref, right[ORDERS[part][2]]))
        go(ag(part, 10 + row, ref, left[ORDERS[part][2]]))
        if row == 3:
            go(across(part, 0, block(c, part, 2, coord(part, 2, 0))))

    def fourth_hop(part):
        axis = ORDERS[part][2]
        before, after = coord(part, 2, SIDE - 1), coord(part, 2, 1)
        for third, slot, sub, peer in ((before, 6, 0, right[axis]), (after, 10, 1, left[axis])):
            for row, by in enumerate((0,) + steps):
                ag(part, slot + row, line(c, part, coord(part, 1, SIDE - by), third), twin).wait_recv()
            go(ag(part, 14 + sub, halved(part, sub, third), peer))
        go(across(part, 1, block(c, part, 2, before)))
        go(across(part, 2, block(c, part, 2, after)))

    def last_hop(part):
        opposite = coord(part, 2, 2)
        ag(part, 14, halved(part, 0, opposite), twin).wait_recv()
        ag(part, 15, halved(part, 1, opposite), twin).wait_recv()
        go(across(part, 3, block(c, part, 2, opposite)))

    def arrived(part, slot):
        value = coord(part, 2, (0, SIDE - 1, 1, 2)[slot])
        across(part, slot, block(other, part, 2, value)).wait_recv()

    early, late = range(3), range(3, 6)
    for part in range(6):
        first_hop(part)
    acc[...] = jnp.zeros_like(acc)
    for wave in (early, late):
        for part in wave:
            second_hop(part)
        for part in wave:
            third_hop(part, 0)
    for wave in (early, late):
        for row in range(1, SIDE):
            for part in wave:
                third_hop(part, row)
    for copy in weights:
        copy.wait()
    for wave in (early, late):
        for part in wave:
            pieces(c, part, coord(part, 2, 0))
    for part in early:
        fourth_hop(part)
    for wave in (early, late):
        for part in wave:
            arrived(part, 0)
            pieces(other, part, coord(part, 2, 0))
    for part in late:
        fourth_hop(part)
    for wave in (early, late):
        for part in wave:
            pieces(c, part, coord(part, 2, 1), coord(part, 2, SIDE - 1))
    for part in early:
        last_hop(part)
    for wave in (early, late):
        for part in wave:
            arrived(part, 1)
            arrived(part, 2)
            pieces(other, part, coord(part, 2, 1), coord(part, 2, SIDE - 1))
    for part in late:
        last_hop(part)
    for wave in (early, late):
        for part in wave:
            pieces(c, part, coord(part, 2, 2))
    for wave in (early, late):
        for part in wave:
            arrived(part, 3)
            pieces(other, part, coord(part, 2, 2))

    first = (c * 8 + g) * experts
    row = lax.broadcasted_iota(jnp.int32, (LANES, hidden_width), 0)
    picks = []
    for j in range(experts):
        e = first + j
        hit = (row == e) | (row == e + 32) | (row == e + 64)
        picks.append(jnp.where(hit, 1.0, 0.0).astype(jnp.bfloat16))
    def act_step(i, carry):
        share = xs[0, i, :, :, :, half:wide].reshape(slab, LANES)
        for j in range(experts):
            at = 2 * j * hidden_width
            gate = acc[i, :, :, :, at : at + hidden_width].reshape(slab, hidden_width)
            up = acc[i, :, :, :, at + hidden_width : at + 2 * hidden_width].reshape(slab, hidden_width)
            weight = jnp.dot(share, picks[j], preferred_element_type=jnp.float32)
            act = gate / (1.0 + jnp.exp(-gate)) * up * weight
            hid[pl.ds(pl.multiple_of(i * slab, slab), slab), j * hidden_width : (j + 1) * hidden_width] = act.astype(
                jnp.bfloat16
            )
        return carry

    lax.fori_loop(0, SIDE, act_step, 0)

    rs_parts = split(SCATTER)

    def down(half_index, part, add):
        low, _, high = rs_parts[part]

        value = hid[...]
        for start in range(low, high, TILE):
            stop = min(start + TILE, high)
            at = (slice(None),) * 4 + (slice(start, stop),)
            got = jnp.dot(value, wd[half_index, :, start:stop], preferred_element_type=jnp.float32)
            if add:
                got += r0[at].reshape(got.shape).astype(jnp.float32)
            ps[(half_index,) + at] = got.astype(jnp.bfloat16).reshape(SIDE, SIDE, SIDE, 8, stop - start)

    def pair(half_index, part):
        low, _, high = rs_parts[part]
        cols = (slice(None),) * 4 + (slice(low, high),)
        return remote(ps.at[(half_index,) + cols], r0.at[cols], pr_s.at[part], pr_r.at[part], twin)

    def plus(index, *others):
        total = ps[index].astype(jnp.float32)
        for value in others:
            total += value.astype(jnp.float32)
        ps[index] = total.astype(jnp.bfloat16)

    def big(part, kind):
        axis = ORDERS[part][2]
        low, cut, high = rs_parts[part]
        by, start, stop, buf, peer = (
            (2, low, cut, fa, right),
            (2, cut, high, fb, left),
            (1, cut, high, rl, right),
            (SIDE - 1, low, cut, rr, left),
            (1, low, cut, rl, right),
            (SIDE - 1, cut, high, rr, left),
        )[kind]
        ref = ps.at[(c,) + spot(part, 2, shifted(axis, by)[axis]) + (slice(start, stop),)]
        dst = buf[part]
        if kind > 1:
            dst = dst.at[:, :, :, start - low : stop - low]
        return remote(ref, dst, rs_s.at[part, kind], rs_r.at[part, kind], peer[axis])

    def small(part, stage, k):
        axis = ORDERS[part][stage]
        low, _, high = rs_parts[part]
        ref = ps.at[(c,) + spot(part, stage, shifted(axis, steps[k])[axis]) + (slice(low, high),)]
        dst = (s0, s1)[stage][part].at[k]
        return remote(
            ref, dst, rs_s.at[part, 6 + 3 * stage + k], rs_r.at[part, 6 + 3 * stage + k], toward[steps[k]][axis]
        )

    def accumulate(part, by, low, high, others):
        axis = ORDERS[part][2]
        base = rs_parts[part][0]
        index = (c,) + spot(part, 2, shifted(axis, by)[axis]) + (slice(low, high),)
        free = [i for i, s in enumerate(index[:-2]) if isinstance(s, slice)][0]

        def step(i, carry):
            inner = tuple(i if k == free else s for k, s in enumerate(index))
            plus(inner, *[o[i, :, :, at : at + high - low] for o, at in others])
            return carry

        lax.fori_loop(0, SIDE, step, 0)

    def forward(part):
        low, cut, high = rs_parts[part]
        big(part, 0).wait_recv()
        accumulate(part, 1, low, cut, [(fa[part], 0)])
        go(big(part, 4))
        big(part, 1).wait_recv()
        accumulate(part, SIDE - 1, cut, high, [(fb[part], 0)])
        go(big(part, 5))

    def settle(part):
        low, cut, high = rs_parts[part]
        for kind in range(2, 6):
            big(part, kind).wait_recv()
        accumulate(part, 0, low, high, [(rl[part], 0), (rr[part], 0)])
        for k in range(3):
            go(small(part, 1, k))

    def finish_axis(part, stage):
        low, cut, high = rs_parts[part]
        for k in range(3):
            small(part, stage, k).wait_recv()
        index = (c,) + spot(part, stage, me[ORDERS[part][stage]]) + (slice(low, high),)
        plus(index, *[(s0, s1)[stage][part][k] for k in range(3)])
        if stage:
            for k in range(3):
                go(small(part, 0, k))

    ahead = 3
    for part in range(ahead):
        down(other, part, False)
        go(pair(other, part))
    for part in range(6):
        if part + ahead < 6:
            down(other, part + ahead, False)
            go(pair(other, part + ahead))
        pair(c, part).wait_recv()
        down(c, part, True)
        for kind in range(4):
            go(big(part, kind))
        if part >= 3:
            forward(part - 3)
    for part in late:
        forward(part)
    for part in range(6):
        settle(part)
    for stage in (1, 0):
        for part in range(6):
            finish_axis(part, stage)

    back = remote(ps.at[(c,) + me], fin, ex_s, ex_r, twin)
    back.start()
    out[:, pl.ds(pl.multiple_of(c * half, half), half)] = ps[(c,) + me]
    back.wait()
    out[:, pl.ds(pl.multiple_of(other * half, half), half)] = fin[...]
    for copy in sent:
        copy.wait_send()


def body(tokens, expert_ids, gate_weights, w_gate, w_up, w_down):
    row_count, model_width = tokens.shape
    half = model_width // 2
    experts, _, hidden_width = w_gate.shape
    c = lax.axis_index("sect")
    wide = half + LANES
    sides = (SIDE,) * 3
    bf16 = jnp.bfloat16
    rs_parts = split(SCATTER)
    plane = (SIDE, SIDE, 8)
    landing = [plane + (cut - lo,) for lo, cut, hi in rs_parts]
    landing += [plane + (hi - cut,) for lo, cut, hi in rs_parts]
    landing += [plane + (hi - lo,) for lo, cut, hi in rs_parts] * 2
    landing += [(3, SIDE, 8, hi - lo) for lo, cut, hi in rs_parts]
    landing += [(3, 8, hi - lo) for lo, cut, hi in rs_parts]
    scratch = [
        pltpu.VMEM((2, 8, wide), bf16),
        pltpu.VMEM((8, wide), bf16),
        pltpu.VMEM((2,) + sides + (8, wide), bf16),
        pltpu.VMEM((2, half, 2 * experts * hidden_width), bf16),
        pltpu.VMEM((2, experts * hidden_width, half), bf16),
        pltpu.VMEM(sides + (8, 2 * experts * hidden_width), jnp.float32),
        pltpu.VMEM((8 * SIDE**3, experts * hidden_width), bf16),
        pltpu.VMEM((2,) + sides + (8, half), bf16),
        pltpu.VMEM(sides + (8, half), bf16),
    ]
    scratch += [pltpu.VMEM(s, bf16) for s in landing]
    scratch += [pltpu.VMEM((8, half), bf16)]
    dma = pltpu.SemaphoreType.DMA
    scratch += [
        dma((2, 3 * experts)),
        dma,
        dma,
        dma((6, 16)),
        dma((6, 16)),
        dma((6, 4)),
        dma((6, 4)),
        dma((6,)),
        dma((6,)),
        dma((6, 12)),
        dma((6, 12)),
    ]
    anywhere = pl.BlockSpec(memory_space=pl.ANY)
    vmem = pl.BlockSpec(memory_space=pltpu.VMEM)
    out = pl.pallas_call(
        functools.partial(kernel, half),
        out_shape=jax.ShapeDtypeStruct((8, model_width), bf16),
        in_specs=[vmem, vmem, vmem, anywhere, anywhere, anywhere],
        out_specs=vmem,
        scratch_shapes=scratch,
        compiler_params=pltpu.CompilerParams(
            collective_id=0, has_side_effects=True, vmem_limit_bytes=60 * 1024 * 1024
        ),
    )(tokens, expert_ids, gate_weights, w_gate, w_up, w_down)
    return lax.dynamic_slice_in_dim(out, c * row_count, row_count, axis=0)


def solution(mesh):
    in_specs = (
        P(ALL, None),
        P(ALL, None),
        P(ALL, None),
        P(("sect", "grp"), None, "dev"),
        P(("sect", "grp"), None, "dev"),
        P(("sect", "grp"), "dev", None),
    )
    return jax.shard_map(body, mesh=mesh, in_specs=in_specs, out_specs=P(ALL, None), check_vma=False)
```

time: 80 us -> 70.3 us (0.88)
  Pallas kernels: 75.7 us -> 68.6 us
  other arithmetic: 2.18 us -> 0 us
    pallas_call x1, Pallas kernels: 75.7 us -> 68.6 us  [body(): pl.pallas_call(functools.partial(kernel, half), out_shape=jax.ShapeDtypeS...]
    dynamic_slice x0 -> x1, local copies, waits for them, and re-layouts: none -> 1.56 us  [body(): return lax.dynamic_slice_in_dim(out, c * row_count, row_count, axis=0)]
    squeeze x1 -> x0, local copies, waits for them, and re-layouts: 0.89 us -> none  [body(): return jnp.concatenate([picked[0], picked[1]], axis=1)]
where the time goes in v3:
time: 70.3 us; the launch traced here: 70.2 us
  Pallas kernels  68.6 us (98%)
  local copies, waits for them, and re-layouts  1.56 us (2%)
    pallas_call x1, Pallas kernels, body(): pl.pallas_call(functools.partial(kernel, half), out_shape=jax.ShapeDtypeS...  68.6 us
    dynamic_slice x1, local copies, waits for them, and re-layouts, body(): return lax.dynamic_slice_in_dim(out, c * row_count, row_count, axis=0)  1.56 us

profile of v3, /device:TPU:1, one launch (start us, length us, event | category | flops | bytes accessed | tf_op | source)
XLA Modules:
  0.0 70.2 jit_solution(1804654458141974899)
XLA Ops:
  0.0 68.6 %shard_map.64 = bf16[8,7168]{1,0:T(8,128)(2,1)} custom-call(bf16[4,7168]{1,0:T(4,128)(2,1)} %tokens.1, s32[4,8]{1,0:T(4,128)} %ids.1, f32[4,8]{1,0:T(4,128)} %shares.1, bf16[2,7168,256]{2,1,0:T(8,128)(2,1)} %wg_hbm.1, bf16[2,7168,256]{2,1,0:T(8,128)(2,1)} %wu_hbm.1, bf16[2,256,7168]{2,1,0:T(8,128)(2,1)} %wd_hbm.1), custom_call_target="tpu_custom_call" | custom-call | tf_op jit(solution)/shard_map/pallas_call | solution.py:443
  68.6 1.6 %constant_dynamic-slice_fusion = bf16[4,7168]{1,0:T(4,128)(2,1)} fusion(bf16[8,7168]{1,0:T(8,128)(2,1)} %shard_map.64, s32[]{:T(128)S(6)} %select_n.3), kind=kLoop, calls=%fused_computation | loop fusion | bytes 114692 | tf_op jit(solution)/shard_map/dynamic_slice | solution.py:453

commit v4 on v3

--- a/solution.py
+++ b/solution.py
@@ -12,11 +12,15 @@
 SIDE = 4
 LANES = 128
 TILE = 256
-ORDERS = ((0, 1, 2), (1, 2, 0), (2, 0, 1)) * 2
-
-
-GATHER = (6, 6, 4, 4, 4, 5)
-SCATTER = (6, 6, 4, 4, 4, 4)
+ORDERS = ((0, 1, 2), (1, 2, 0), (2, 0, 1)) * 3
+WAVES = (range(0, 3), range(3, 6), range(0))
+PARTS = 6
+AHEAD = 3
+LAG = 6
+
+
+GATHER = (6, 6, 6, 4, 4, 3)
+SCATTER = (6, 6, 6, 4, 4, 2)
 
 
 def split(counts):
@@ -30,9 +34,9 @@
 
 
 def kernel(half, tokens, ids, shares, wg_hbm, wu_hbm, wd_hbm, out, t8, tr, xs, wall, wd, acc, hid, ps, r0, *rest):
-    fa, fb, rl, rr, s1, s0 = (rest[i : i + 6] for i in range(0, 36, 6))
-    fin = rest[36]
-    wsem, ex_s, ex_r, ag_s, ag_r, dd_s, dd_r, pr_s, pr_r, rs_s, rs_r = rest[37:]
+    fa, fb, rl, rr, s1, s0 = (rest[i : i + PARTS] for i in range(0, 6 * PARTS, PARTS))
+    fin = rest[6 * PARTS]
+    wsem, ex_s, ex_r, ag_s, ag_r, dd_s, dd_r, pr_s, pr_r, rs_s, rs_r, fin_s, fin_r = rest[6 * PARTS + 1 :]
     wide = half + LANES
     experts = wg_hbm.shape[0]
     hidden_width = wg_hbm.shape[2]
@@ -52,9 +56,10 @@
     left = [device(shifted(a, SIDE - 1), c) for a in range(3)]
     far = [device(shifted(a, 2), c) for a in range(3)]
     toward = {1: right, 2: far, 3: left}
+    cross = {by: [device(shifted(a, by), other) for a in range(3)] for by in (1, 2, 3)}
 
     barrier = pltpu.get_barrier_semaphore()
-    for peer in [twin] + right + left + far:
+    for peer in [twin] + right + left + far + cross[1] + cross[2] + cross[3]:
         pl.semaphore_signal(barrier, inc=1, device_id=peer, device_id_type=MESH)
 
     weights = []
@@ -92,7 +97,7 @@
             eight = jnp.concatenate([value, value], axis=0)
             owner = lax.broadcasted_iota(jnp.int32, eight.shape, 0) // 4
             t8[h, :, low:high] = jnp.where(owner == c, eight, 0.0).astype(jnp.bfloat16)
-    pl.semaphore_wait(barrier, 10)
+    pl.semaphore_wait(barrier, 19)
 
     def remote(src, dst, send, recv, peer):
         return pltpu.make_async_remote_copy(
@@ -206,51 +211,67 @@
         value = coord(part, 2, (0, SIDE - 1, 1, 2)[slot])
         across(part, slot, block(other, part, 2, value)).wait_recv()
 
-    early, late = range(3), range(3, 6)
-    for part in range(6):
-        first_hop(part)
+    def near(core_half, wave):
+        for part in wave:
+            if core_half is other:
+                arrived(part, 0)
+            pieces(core_half, part, coord(part, 2, 0))
+
+    def beside(core_half, wave):
+        for part in wave:
+            if core_half is other:
+                arrived(part, 1)
+                arrived(part, 2)
+            pieces(core_half, part, coord(part, 2, 1), coord(part, 2, SIDE - 1))
+
+    def opposite(core_half, wave):
+        for part in wave:
+            if core_half is other:
+                arrived(part, 3)
+            pieces(core_half, part, coord(part, 2, 2))
+
+    def each(step, wave):
+        for part in wave:
+            step(part)
+
+    for wave in WAVES:
+        each(first_hop, wave)
     acc[...] = jnp.zeros_like(acc)
-    for wave in (early, late):
-        for part in wave:
-            second_hop(part)
+    for wave in WAVES:
+        each(second_hop, wave)
         for part in wave:
             third_hop(part, 0)
-    for wave in (early, late):
+    for wave in WAVES:
         for row in range(1, SIDE):
             for part in wave:
                 third_hop(part, row)
     for copy in weights:
         copy.wait()
-    for wave in (early, late):
-        for part in wave:
-            pieces(c, part, coord(part, 2, 0))
-    for part in early:
-        fourth_hop(part)
-    for wave in (early, late):
-        for part in wave:
-            arrived(part, 0)
-            pieces(other, part, coord(part, 2, 0))
-    for part in late:
-        fourth_hop(part)
-    for wave in (early, late):
-        for part in wave:
-            pieces(c, part, coord(part, 2, 1), coord(part, 2, SIDE - 1))
-    for part in early:
-        last_hop(part)
-    for wave in (early, late):
-        for part in wave:
-            arrived(part, 1)
-            arrived(part, 2)
-            pieces(other, part, coord(part, 2, 1), coord(part, 2, SIDE - 1))
-    for part in late:
-        last_hop(part)
-    for wave in (early, late):
-        for part in wave:
-            pieces(c, part, coord(part, 2, 2))
-    for wave in (early, late):
-        for part in wave:
-            arrived(part, 3)
-            pieces(other, part, coord(part, 2, 2))
+    w0, w1, w2 = WAVES
+    near(c, w0)
+    near(c, w1)
+    each(fourth_hop, w0)
+    near(c, w2)
+    near(other, w0)
+    near(other, w1)
+    each(fourth_hop, w1)
+    near(other, w2)
+    beside(c, w0)
+    each(fourth_hop, w2)
+    beside(other, w0)
+    each(last_hop, w0)
+    beside(c, w1)
+    beside(other, w1)
+    each(last_hop, w1)
+    beside(c, w2)
+    opposite(c, w0)
+    each(last_hop, w2)
+    beside(other, w2)
+    opposite(other, w0)
+    opposite(c, w1)
+    opposite(other, w1)
+    opposite(c, w2)
+    opposite(other, w2)
 
     first = (c * 8 + g) * experts
     row = lax.broadcasted_iota(jnp.int32, (LANES, hidden_width), 0)
@@ -325,6 +346,14 @@
             ref, dst, rs_s.at[part, 6 + 3 * stage + k], rs_r.at[part, 6 + 3 * stage + k], toward[steps[k]][axis]
         )
 
+    def swapped(part, k):
+        axis = ORDERS[part][0]
+        low, _, high = rs_parts[part]
+        peer = cross[steps[k]][axis] if k < 3 else twin
+        by = steps[k] if k < 3 else 0
+        ref = ps.at[(c,) + spot(part, 0, shifted(axis, by)[axis]) + (slice(low, high),)]
+        return remote(ref, fin.at[k, :, low:high], fin_s.at[part, k], fin_r.at[part, k], peer)
+
     def accumulate(part, by, low, high, others):
         axis = ORDERS[part][2]
         base = rs_parts[part][0]
@@ -360,38 +389,55 @@
         for k in range(3):
             small(part, stage, k).wait_recv()
         index = (c,) + spot(part, stage, me[ORDERS[part][stage]]) + (slice(low, high),)
-        plus(index, *[(s0, s1)[stage][part][k] for k in range(3)])
+        if stage == 0:
+            total = ps[index].astype(jnp.float32)
+            for k in range(3):
+                total += s0[part][k].astype(jnp.float32)
+            out[:, pl.ds(pl.multiple_of(c * half + low, LANES), high - low)] = total.astype(jnp.bfloat16)
+            total = jnp.zeros((8, high - low), jnp.float32)
+            for k in range(4):
+                swapped(part, k).wait_recv()
+                total += fin[k, :, low:high].astype(jnp.float32)
+            out[:, pl.ds(pl.multiple_of(other * half + low, LANES), high - low)] = total.astype(jnp.bfloat16)
+            return
+        plus(index, *[s1[part][k] for k in range(3)])
         if stage:
             for k in range(3):
                 go(small(part, 0, k))
-
-    ahead = 3
-    for part in range(ahead):
+                go(swapped(part, k))
+            go(swapped(part, 3))
+
+    for part in range(AHEAD):
         down(other, part, False)
         go(pair(other, part))
-    for part in range(6):
-        if part + ahead < 6:
-            down(other, part + ahead, False)
-            go(pair(other, part + ahead))
+    for part in range(PARTS):
+        if part + AHEAD < PARTS:
+            down(other, part + AHEAD, False)
+            go(pair(other, part + AHEAD))
         pair(c, part).wait_recv()
         down(c, part, True)
         for kind in range(4):
             go(big(part, kind))
-        if part >= 3:
-            forward(part - 3)
-    for part in late:
+        if part >= LAG:
+            forward(part - LAG)
+    for part in range(PARTS - LAG, PARTS):
         forward(part)
-    for part in range(6):
-        settle(part)
-    for stage in (1, 0):
-        for part in range(6):
-            finish_axis(part, stage)
-
-    back = remote(ps.at[(c,) + me], fin, ex_s, ex_r, twin)
-    back.start()
-    out[:, pl.ds(pl.multiple_of(c * half, half), half)] = ps[(c,) + me]
-    back.wait()
-    out[:, pl.ds(pl.multiple_of(other * half, half), half)] = fin[...]
+    each(settle, w0)
+    each(settle, w1)
+    for part in w0:
+        finish_axis(part, 1)
+    each(settle, w2)
+    for part in w1:
+        finish_axis(part, 1)
+    for part in w0:
+        finish_axis(part, 0)
+    for part in w2:
+        finish_axis(part, 1)
+    for part in w1:
+        finish_axis(part, 0)
+    for part in w2:
+        finish_axis(part, 0)
+
     for copy in sent:
         copy.wait_send()
 
@@ -423,20 +469,22 @@
         pltpu.VMEM(sides + (8, half), bf16),
     ]
     scratch += [pltpu.VMEM(s, bf16) for s in landing]
-    scratch += [pltpu.VMEM((8, half), bf16)]
+    scratch += [pltpu.VMEM((4, 8, half), bf16)]
     dma = pltpu.SemaphoreType.DMA
     scratch += [
         dma((2, 3 * experts)),
         dma,
         dma,
-        dma((6, 16)),
-        dma((6, 16)),
-        dma((6, 4)),
-        dma((6, 4)),
-        dma((6,)),
-        dma((6,)),
-        dma((6, 12)),
-        dma((6, 12)),
+        dma((PARTS, 16)),
+        dma((PARTS, 16)),
+        dma((PARTS, 4)),
+        dma((PARTS, 4)),
+        dma((PARTS,)),
+        dma((PARTS,)),
+        dma((PARTS, 12)),
+        dma((PARTS, 12)),
+        dma((PARTS, 4)),
+        dma((PARTS, 4)),
     ]
     anywhere = pl.BlockSpec(memory_space=pl.ANY)
     vmem = pl.BlockSpec(memory_space=pltpu.VMEM)

time: 70.3 us -> 69.3 us (0.986)
  Pallas kernels: 68.6 us -> 67.5 us
    pallas_call x1, Pallas kernels: 68.6 us -> 67.5 us  [body(): pl.pallas_call(functools.partial(kernel, half), out_shape=jax.ShapeDtypeS...]
where the time goes in v4:
time: 69.3 us; the launch traced here: 69.1 us
  Pallas kernels  67.5 us (97%)
  local copies, waits for them, and re-layouts  1.56 us (2%)
    pallas_call x1, Pallas kernels, body(): pl.pallas_call(functools.partial(kernel, half), out_shape=jax.ShapeDtypeS...  67.5 us
    dynamic_slice x1, local copies, waits for them, and re-layouts, body(): return lax.dynamic_slice_in_dim(out, c * row_count, row_count, axis=0)  1.56 us

profile of v4, /device:TPU:1, one launch (start us, length us, event | category | flops | bytes accessed | tf_op | source)
XLA Modules:
  0.0 69.1 jit_solution(3075796015671584210)
XLA Ops:
  0.0 67.5 %shard_map.64 = bf16[8,7168]{1,0:T(8,128)(2,1)} custom-call(bf16[4,7168]{1,0:T(4,128)(2,1)} %tokens.1, s32[4,8]{1,0:T(4,128)} %ids.1, f32[4,8]{1,0:T(4,128)} %shares.1, bf16[2,7168,256]{2,1,0:T(8,128)(2,1)} %wg_hbm.1, bf16[2,7168,256]{2,1,0:T(8,128)(2,1)} %wu_hbm.1, bf16[2,256,7168]{2,1,0:T(8,128)(2,1)} %wd_hbm.1), custom_call_target="tpu_custom_call" | custom-call | tf_op jit(solution)/shard_map/pallas_call | solution.py:491
  67.5 1.6 %constant_dynamic-slice_fusion = bf16[4,7168]{1,0:T(4,128)(2,1)} fusion(bf16[8,7168]{1,0:T(8,128)(2,1)} %shard_map.64, s32[]{:T(128)S(6)} %select_n.3), kind=kLoop, calls=%fused_computation | loop fusion | bytes 114692 | tf_op jit(solution)/shard_map/dynamic_slice | solution.py:501

commit v5 on v4

--- a/solution.py
+++ b/solution.py
@@ -15,7 +15,7 @@
 ORDERS = ((0, 1, 2), (1, 2, 0), (2, 0, 1)) * 3
 WAVES = (range(0, 3), range(3, 6), range(0))
 PARTS = 6
-AHEAD = 3
+AHEAD = 2
 LAG = 6
 
 

time: 69.3 us -> 69.4 us (level)
  no operation moved by 1% of the time
where the time goes in v5:
time: 69.4 us; the launch traced here: 69.2 us
  Pallas kernels  67.6 us (97%)
  local copies, waits for them, and re-layouts  1.56 us (2%)
    pallas_call x1, Pallas kernels, body(): pl.pallas_call(functools.partial(kernel, half), out_shape=jax.ShapeDtypeS...  67.6 us
    dynamic_slice x1, local copies, waits for them, and re-layouts, body(): return lax.dynamic_slice_in_dim(out, c * row_count, row_count, axis=0)  1.56 us

profile of v5, /device:TPU:1, one launch (start us, length us, event | category | flops | bytes accessed | tf_op | source)
XLA Modules:
  0.0 69.2 jit_solution(2516138693578067563)
XLA Ops:
  0.0 67.6 %shard_map.64 = bf16[8,7168]{1,0:T(8,128)(2,1)} custom-call(bf16[4,7168]{1,0:T(4,128)(2,1)} %tokens.1, s32[4,8]{1,0:T(4,128)} %ids.1, f32[4,8]{1,0:T(4,128)} %shares.1, bf16[2,7168,256]{2,1,0:T(8,128)(2,1)} %wg_hbm.1, bf16[2,7168,256]{2,1,0:T(8,128)(2,1)} %wu_hbm.1, bf16[2,256,7168]{2,1,0:T(8,128)(2,1)} %wd_hbm.1), custom_call_target="tpu_custom_call" | custom-call | tf_op jit(solution)/shard_map/pallas_call | solution.py:491
  67.6 1.6 %constant_dynamic-slice_fusion = bf16[4,7168]{1,0:T(4,128)(2,1)} fusion(bf16[8,7168]{1,0:T(8,128)(2,1)} %shard_map.64, s32[]{:T(128)S(6)} %select_n.3), kind=kLoop, calls=%fused_computation | loop fusion | bytes 114692 | tf_op jit(solution)/shard_map/dynamic_slice | solution.py:501
